TPU v7x, 32 devices: a whole 2x2x4 slice. The times are simulated.
32 devices in a mesh: pix: 16 (over z, x, core), rep: 2 (over y).
Axes of the slice: x: 2, y: 2, z: 4, core: 2. Of those that a mesh axis runs over, the one named last changes fastest.
Arguments:
- tokens: bfloat16 [256, 16, 1152], P(('pix', 'rep')), may hold values from -48 to 48
- out_grad: bfloat16 [256, 16, 1152], P(('pix', 'rep')), may hold values from -6 to 6
- query_weight: bfloat16 [1152, 1152], P('pix'), may hold values from -0.1875 to 0.1875
- key_weight: bfloat16 [1152, 1152], P('pix'), may hold values from -0.1875 to 0.1875
- value_weight: bfloat16 [1152, 1152], P('pix'), may hold values from -0.1875 to 0.1875
- output_weight: bfloat16 [1152, 1152], P('pix'), may hold values from -0.1875 to 0.1875
Outputs:
- input_grad: bfloat16 [256, 16, 1152], P(('pix', 'rep'))
- weight_grads: float32 [1152, 4608], P('pix')
All inputs are finite; a program needn't handle non-finite values.
Results may differ from a plain program's by a relative error of at most 0.025.
The roundings to bfloat16 on the way count: a program that leaves them out, or rounds other values in their place, can miss the bound.
Values may be sent and summed in bfloat16 or wider, within the bound.
No kernel may reach another device: no remote copies, remote signals or barrier semaphores. Data moves between devices by JAX's collectives and lax.ppermute only.
A program may use at most 128 MiB of HBM per device.

v0:
```python
import jax
import jax.numpy as jnp
from jax import lax
from jax.sharding import PartitionSpec as P

D = 1152
HEADS = 16
HEAD_DIM = 72
FRAMES = 16


def contract_last(left, right):
    return lax.dot_general(
        left, right, (((1,), (1,)), ((), ())), preferred_element_type=jnp.float32
    )


def contract_first(left, right):
    return lax.dot_general(
        left, right, (((0,), (0,)), ((), ())), preferred_element_type=jnp.float32
    )


def local(tokens, out_grad, query_weight, key_weight, value_weight, output_weight):
    count = tokens.shape[0]
    rows = tokens.reshape(-1, D)
    drows = out_grad.reshape(-1, D)
    scale = 1.0 / HEAD_DIM**0.5
    full_q, full_k, full_v = (
        lax.all_gather(query_weight, "pix", axis=0, tiled=True),
        lax.all_gather(key_weight, "pix", axis=0, tiled=True),
        lax.all_gather(value_weight, "pix", axis=0, tiled=True),
    )
    query = jnp.dot(rows, full_q, preferred_element_type=jnp.float32).astype(jnp.bfloat16)
    keyed = jnp.dot(rows, full_k, preferred_element_type=jnp.float32).astype(jnp.bfloat16)
    valued = jnp.dot(rows, full_v, preferred_element_type=jnp.float32).astype(jnp.bfloat16)
    shape4 = (count, FRAMES, HEADS, HEAD_DIM)
    qh = query.reshape(shape4)
    kh = keyed.reshape(shape4)
    vh = valued.reshape(shape4)
    scores = jnp.einsum("sfhe,sghe->shfg", qh, kh, preferred_element_type=jnp.float32) * scale
    scores = scores - jnp.max(scores, axis=-1, keepdims=True)
    expo = jnp.exp(scores)
    probs = expo / jnp.sum(expo, axis=-1, keepdims=True)
    probs_b = probs.astype(jnp.bfloat16)
    attended = (
        jnp.einsum("shfg,sghe->sfhe", probs_b, vh, preferred_element_type=jnp.float32)
        .reshape(-1, D)
        .astype(jnp.bfloat16)
    )
    output_full = lax.all_gather(output_weight, "pix", axis=0, tiled=True)
    dattn = contract_last(drows, output_full).astype(jnp.bfloat16)
    dah = dattn.reshape(shape4)
    dvalue = (
        jnp.einsum("shfg,sfhe->sghe", probs_b, dah, preferred_element_type=jnp.float32)
        .reshape(-1, D)
        .astype(jnp.bfloat16)
    )
    dprobs = jnp.einsum("sfhe,sghe->shfg", dah, vh, preferred_element_type=jnp.float32)
    dscore = (probs * (dprobs - jnp.sum(dprobs * probs, axis=-1, keepdims=True)) * scale).astype(
        jnp.bfloat16
    )
    dquery = (
        jnp.einsum("shfg,sghe->sfhe", dscore, kh, preferred_element_type=jnp.float32)
        .reshape(-1, D)
        .astype(jnp.bfloat16)
    )
    dkey = (
        jnp.einsum("shfg,sfhe->sghe", dscore, qh, preferred_element_type=jnp.float32)
        .reshape(-1, D)
        .astype(jnp.bfloat16)
    )
    grads = lax.psum_scatter(
        jnp.concatenate(
            [
                jnp.concatenate(
                    [
                        contract_first(rows, dquery),
                        contract_first(rows, dkey),
                        contract_first(rows, dvalue),
                    ],
                    axis=1,
                ),
                contract_first(attended, drows),
            ],
            axis=1,
        ).astype(jnp.bfloat16),
        "pix",
        scatter_dimension=0,
        tiled=True,
    ).astype(jnp.float32)
    back_q, back_k, back_v = (
        lax.all_gather(query_weight, "pix", axis=0, tiled=True),
        lax.all_gather(key_weight, "pix", axis=0, tiled=True),
        lax.all_gather(value_weight, "pix", axis=0, tiled=True),
    )
    dinput = (
        contract_last(dquery, back_q) + contract_last(dkey, back_k) + contract_last(dvalue, back_v)
    )
    weight_grads = lax.psum(grads, "rep")
    return (dinput.astype(jnp.bfloat16).reshape(tokens.shape), weight_grads)


def solution(mesh):
    placed = (
        P(("pix", "rep"), None, None),
        P(("pix", "rep"), None, None),
        P("pix", None),
        P("pix", None),
        P("pix", None),
        P("pix", None),
    )
    return jax.shard_map(
        local,
        mesh=mesh,
        in_specs=placed,
        out_specs=(P(("pix", "rep"), None, None), P("pix", None)),
        check_vma=False,
    )
```

profile of v0, /device:TPU:0, one launch (start us, length us, event | category | flops | bytes accessed | tf_op | source)
XLA Modules:
  0.0 441.2 jit_solution(11428805849281007432)
XLA Ops:
  7.2 0.7 all-gather.9.cloned.1.call-update
  7.9 0.0 all-gather.11.cloned.1.call-start
  8.0 0.7 all-gather.11.cloned.1.call-update
  8.7 0.7 all-gather.5.cloned.1.call-update
  9.4 0.5 all-gather.7.cloned.1.call-update
  10.0 0.0 reduce-scatter.4.cloned.1.call-start
  10.0 46.1 %all-gather.9.cloned.1.call-done = bf16[1152,1152]{1,0:T(8,128)(2,1)} async-done(((bf16[72,1152]{1,0:T(8,128)(2,1)}), bf16[1152,1152]{1,0:T(8,128)(2,1)}) %all-gather.9.cloned.1.call-update) | async-done | bytes 2654224 | tf_op jit(solution)/shard_map/all_gather | solution.py:51
  56.1 2.8 convolution_convert_fusion.5
  58.9 0.9 reshape.43
  59.8 40.5 %all-gather.11.cloned.1.call-done = bf16[1152,1152]{1,0:T(8,128)(2,1)} async-done(((bf16[72,1152]{1,0:T(8,128)(2,1)}), bf16[1152,1152]{1,0:T(8,128)(2,1)}) %all-gather.11.cloned.1.call-update) | async-done | bytes 2654224 | tf_op jit(solution)/shard_map/all_gather | solution.py:32
  100.3 2.3 convolution_convert_fusion.4
  102.6 0.9 reshape.44
  103.6 40.9 %all-gather.5.cloned.1.call-done = bf16[1152,1152]{1,0:T(8,128)(2,1)} async-done(((bf16[72,1152]{1,0:T(8,128)(2,1)}), bf16[1152,1152]{1,0:T(8,128)(2,1)}) %all-gather.5.cloned.1.call-update) | async-done | bytes 2654224 | tf_op jit(solution)/shard_map/all_gather | solution.py:31
  144.5 2.3 convolution_convert_fusion.7
  146.8 0.9 reshape.40
  147.8 40.8 %all-gather.7.cloned.1.call-done = bf16[1152,1152]{1,0:T(8,128)(2,1)} async-done(((bf16[72,1152]{1,0:T(8,128)(2,1)}), bf16[1152,1152]{1,0:T(8,128)(2,1)}) %all-gather.7.cloned.1.call-update) | async-done | bytes 2654224 | tf_op jit(solution)/shard_map/all_gather | solution.py:30
  188.6 2.3 convolution_convert_fusion.6
  190.9 0.9 reshape.41
  191.9 0.4 fusion.26
  192.3 1.7 fusion.48
  194.0 2.3 fusion.14
  196.3 2.3 fusion.13
  198.6 3.0 fusion.12
  201.6 1.6 fusion.15
  203.3 0.1 copy.44
  203.4 0.5 convert_element_type.81
  204.0 0.1 copy.47
  204.1 0.5 convert_element_type.85
  204.6 0.1 copy.40
  204.8 0.5 convert_element_type.74
  205.3 0.1 copy.42
  205.4 0.5 convert_element_type.77
  205.9 0.9 fusion.4
  206.8 0.9 fusion.3
  207.7 0.9 fusion.2
  208.8 0.9 convolution_convert_fusion
  209.7 28.0 %pad_maximum_fusion = bf16[1152,4608]{0,1:T(8,128)(2,1)} fusion(bf16[1152,1152]{0,1:T(8,128)(2,1)S(1)} %convolution_convert_fusion, bf16[1152,1152]{0,1:T(8,128)(2,1)S(1)} %fusion.4, bf16[1152,1152]{0,1:T(8,128)(2,1)S(1)} %fusion.3, bf16[1152,1152]{0,1:T(8,128)(2,1)S(1)} %fusion.2), kind=kLoop, calls=%fused_computation.2 | loop fusion | flops 42467328 | bytes 21233664 | tf_op jit(solution)/shard_map/concatenate | solution.py:74
  237.7 15.3 %copy.51 = bf16[1152,4608]{1,0:T(8,128)(2,1)} copy(bf16[1152,4608]{0,1:T(8,128)(2,1)} %pad_maximum_fusion) | data formatting | bytes 21233664
  253.0 1.7 copy-done.2
  254.7 0.9 fusion.53
  255.7 0.8 copy-done.1
  256.5 0.9 convolution_add_fusion.1
  257.4 1.2 copy-done.3
  258.7 1.6 fusion.5
  260.3 112.4 %reduce-scatter.4.cloned.1.call-done = bf16[72,4608]{1,0:T(8,128)(2,1)} async-done(((bf16[1152,4608]{1,0:T(8,128)(2,1)}), bf16[72,4608]{1,0:T(8,128)(2,1)}) %reduce-scatter.4.cloned.1.call-update) | async-done | bytes 663568
  372.7 2.3 copy.52
  375.0 57.9 %all-reduce.1 = f32[72,4608]{0,1:T(8,128)S(1)} all-reduce(bf16[72,4608]{0,1:T(8,128)(2,1)} %copy.52), channel_id=1, replica_groups=mesh['pix'=16,'rep'=2] {'rep'}, use_global_device_ids=true, to_apply=%region_4.0 | all-reduce | flops 331776 | bytes 1990656 | tf_op jit(solution)/shard_map/psum | solution.py:100
  432.9 1.7 copy.48
  (21 shorter events, 0.2 us)
Async XLA Ops:
  7.2 93.1 %copy-start = (bf16[8,16,1152]{2,1,0:T(8,128)(2,1)S(1)}, bf16[8,16,1152]{2,1,0:T(8,128)(2,1)}, u32[]{:S(2)}) copy-start(bf16[8,16,1152]{2,1,0:T(8,128)(2,1)} %param.6) | copy-start | bytes 884740
  7.2 48.9 %all-gather.9.cloned.1.call-start = ((), (), s32[]{:S(2)}) async-start(), calls=%async_computation.3 | async-start | bytes 2820096 | tf_op jit(solution)/shard_map/all_gather | solution.py:51
  7.9 92.4 %all-gather.11.cloned.1.call-start = ((), (), s32[]{:S(2)}) async-start(), calls=%async_computation.4 | async-start | bytes 2820096 | tf_op jit(solution)/shard_map/all_gather | solution.py:32
  8.7 135.8 %all-gather.5.cloned.1.call-start = ((), (), s32[]{:S(2)}) async-start(), calls=%async_computation.1 | async-start | bytes 2820096 | tf_op jit(solution)/shard_map/all_gather | solution.py:31
  9.4 179.2 %all-gather.7.cloned.1.call-start = ((), (), s32[]{:S(2)}) async-start(), calls=%async_computation.2 | async-start | bytes 2820096 | tf_op jit(solution)/shard_map/all_gather | solution.py:30
  10.0 362.7 %reduce-scatter.4.cloned.1.call-start = ((), (), s32[]{:S(2)}) async-start(), calls=%async_computation.5 | async-start | bytes 11280384
  191.9 2.1 copy-start.9
  201.6 1.7 copy-start.8
  203.3 1.3 copy-start.7
  203.9 2.0 copy-start.4
  206.8 1.8 copy-start.6
  253.0 1.7 copy-start.2
  254.7 1.7 copy-start.1
  256.5 2.2 copy-start.3
  256.5 2.2 copy-start.5
Sparse Core Ops, SparseCore 0:
  10.1 45.8 all-gather.8
  58.2 42.0 all-gather.10
  102.4 42.0 all-gather.4
  146.5 42.0 all-gather.6
  253.1 119.5 reduce-scatter.3
where the time goes:
time: 442 us; the launch traced here: 441 us
  waiting for transfers between devices  283 us (64%)
  blocking collectives  57.9 us (13%)
  local copies, waits for them, and re-layouts  29.5 us (7%)
  matrix products  28.1 us (6%)
  other arithmetic  28 us (6%)
  between operations  14.2 us (3%)
    unnamed x6, waiting for transfers between devices  115 us
    psum x1, blocking collectives, local(): weight_grads = lax.psum(grads, 'rep')  57.9 us
    all_gather x1, waiting for transfers between devices, local(): output_full = lax.all_gather(output_weight, 'pix', axis=0, tiled=True)  46.1 us
    all_gather x1, waiting for transfers between devices, local(): lax.all_gather(key_weight, 'pix', axis=0, tiled=True)  40.9 us
    all_gather x1, waiting for transfers between devices, local(): lax.all_gather(query_weight, 'pix', axis=0, tiled=True)  40.8 us
    all_gather x1, waiting for transfers between devices, local(): lax.all_gather(value_weight, 'pix', axis=0, tiled=True)  40.5 us
    concatenate x1, other arithmetic, local(): jnp.concatenate([jnp.concatenate([contract_first(rows, dquery), contract_...  28 us
    unnamed x23, local copies, waits for them, and re-layouts  23.2 us
  transfers between devices with their start and end apart: 5, of which 5 were waited for; matrix products, arithmetic and copies ran while one was open for 3% of the time, Pallas kernels for 0%

commit v1 on v0

--- a/solution.py
+++ b/solution.py
@@ -48,7 +48,13 @@
         .reshape(-1, D)
         .astype(jnp.bfloat16)
     )
-    output_full = lax.all_gather(output_weight, "pix", axis=0, tiled=True)
+    n_dev = lax.axis_size("pix")
+    block, blocks = (output_weight, [output_weight])
+    for _ in range(n_dev - 1):
+        block = lax.ppermute(block, "pix", [(i, (i + 1) % n_dev) for i in range(n_dev)])
+        blocks.insert(0, block)
+    line = jnp.concatenate(blocks, axis=0)
+    output_full = jnp.roll(line, (lax.axis_index("pix") + 1) * output_weight.shape[0], axis=0)
     dattn = contract_last(drows, output_full).astype(jnp.bfloat16)
     dah = dattn.reshape(shape4)
     dvalue = (

time: 442 us -> 426 us (0.964)
  waiting for transfers between devices: 283 us -> 264 us
    ppermute x0 -> x15, waiting for transfers between devices: none -> 121 us  [local(): lax.ppermute(block, 'pix', [(i, (i + 1) % n_dev) for i in range(n_dev)])]
    all_gather x1 -> x0, waiting for transfers between devices: 46.1 us -> none  [local(): output_full = lax.all_gather(output_weight, 'pix', axis=0, tiled=True)]
    all_gather x1, waiting for transfers between devices: 40.9 us -> 0.02 us  [local(): lax.all_gather(key_weight, 'pix', axis=0, tiled=True)]
    all_gather x1, waiting for transfers between devices: 40.5 us -> 0.02 us  [local(): lax.all_gather(value_weight, 'pix', axis=0, tiled=True)]
    all_gather x1, waiting for transfers between devices: 40.8 us -> 27.5 us  [local(): lax.all_gather(query_weight, 'pix', axis=0, tiled=True)]
    unnamed x23 -> x50, local copies, waits for them, and re-layouts: 23.2 us -> 20 us
    unnamed x6 -> x5, waiting for transfers between devices: 115 us -> 116 us
  transfers between devices with their start and end apart: 5 -> 19, of which waited for: 5 -> 17; matrix products, arithmetic and copies ran while one was open for 3% -> 3% of each run, Pallas kernels for 0% -> 0%
where the time goes in v1:
time: 426 us; the launch traced here: 425 us
  waiting for transfers between devices  264 us (62%)
  blocking collectives  57.9 us (14%)
  matrix products  30.2 us (7%)
  local copies, waits for them, and re-layouts  29.5 us (7%)
  other arithmetic  28 us (7%)
  between operations  14.3 us (3%)
    ppermute x15, waiting for transfers between devices, local(): lax.ppermute(block, 'pix', [(i, (i + 1) % n_dev) for i in range(n_dev)])  121 us
    unnamed x5, waiting for transfers between devices  116 us
    psum x1, blocking collectives, local(): weight_grads = lax.psum(grads, 'rep')  57.9 us
    concatenate x1, other arithmetic, local(): jnp.concatenate([jnp.concatenate([contract_first(rows, dquery), contract_...  28 us
    all_gather x1, waiting for transfers between devices, local(): lax.all_gather(query_weight, 'pix', axis=0, tiled=True)  27.5 us
    unnamed x50, local copies, waits for them, and re-layouts  20 us
  transfers between devices with their start and end apart: 19, of which 17 were waited for; matrix products, arithmetic and copies ran while one was open for 3% of the time, Pallas kernels for 0%

profile of v1, /device:TPU:0, one launch (start us, length us, event | category | flops | bytes accessed | tf_op | source)
XLA Modules:
  0.0 424.7 jit_solution(16417071076089501022)
XLA Ops:
  7.2 0.7 all-gather.8.cloned.1.call-update
  8.0 0.7 all-gather.4.cloned.1.call-update
  8.7 0.5 collective-permute-start
  9.3 8.2 %collective-permute-done = bf16[72,1152]{1,0:T(8,128)(2,1)S(1)} collective-permute-done((bf16[72,1152]{1,0:T(8,128)(2,1)}, bf16[72,1152]{1,0:T(8,128)(2,1)S(1)}, u32[]{:S(2)}, u32[]{:S(2)}) %collective-permute-start) | collective-permute-done | bytes 165920 | tf_op jit(solution)/shard_map/ppermute | solution.py:54
  17.5 7.6 %collective-permute-done.1 = bf16[72,1152]{1,0:T(8,128)(2,1)S(1)} collective-permute-done((bf16[72,1152]{1,0:T(8,128)(2,1)S(1)}, bf16[72,1152]{1,0:T(8,128)(2,1)S(1)}, u32[]{:S(2)}, u32[]{:S(2)}) %collective-permute-start.1) | collective-permute-done | bytes 165920 | tf_op jit(solution)/shard_map/ppermute | solution.py:54
  25.0 8.8 %collective-permute-done.2 = bf16[72,1152]{1,0:T(8,128)(2,1)S(1)} collective-permute-done((bf16[72,1152]{1,0:T(8,128)(2,1)S(1)}, bf16[72,1152]{1,0:T(8,128)(2,1)S(1)}, u32[]{:S(2)}, u32[]{:S(2)}) %collective-permute-start.2) | collective-permute-done | bytes 165920 | tf_op jit(solution)/shard_map/ppermute | solution.py:54
  33.8 7.5 %collective-permute-done.3 = bf16[72,1152]{1,0:T(8,128)(2,1)S(1)} collective-permute-done((bf16[72,1152]{1,0:T(8,128)(2,1)S(1)}, bf16[72,1152]{1,0:T(8,128)(2,1)S(1)}, u32[]{:S(2)}, u32[]{:S(2)}) %collective-permute-start.3) | collective-permute-done | bytes 165920 | tf_op jit(solution)/shard_map/ppermute | solution.py:54
  41.3 10.0 %collective-permute-done.4 = bf16[72,1152]{1,0:T(8,128)(2,1)S(1)} collective-permute-done((bf16[72,1152]{1,0:T(8,128)(2,1)S(1)}, bf16[72,1152]{1,0:T(8,128)(2,1)S(1)}, u32[]{:S(2)}, u32[]{:S(2)}) %collective-permute-start.4) | collective-permute-done | bytes 165920 | tf_op jit(solution)/shard_map/ppermute | solution.py:54
  51.3 8.2 %collective-permute-done.5 = bf16[72,1152]{1,0:T(8,128)(2,1)S(1)} collective-permute-done((bf16[72,1152]{1,0:T(8,128)(2,1)S(1)}, bf16[72,1152]{1,0:T(8,128)(2,1)S(1)}, u32[]{:S(2)}, u32[]{:S(2)}) %collective-permute-start.5) | collective-permute-done | bytes 165920 | tf_op jit(solution)/shard_map/ppermute | solution.py:54
  59.5 7.5 %collective-permute-done.6 = bf16[72,1152]{1,0:T(8,128)(2,1)S(1)} collective-permute-done((bf16[72,1152]{1,0:T(8,128)(2,1)S(1)}, bf16[72,1152]{1,0:T(8,128)(2,1)S(1)}, u32[]{:S(2)}, u32[]{:S(2)}) %collective-permute-start.6) | collective-permute-done | bytes 165920 | tf_op jit(solution)/shard_map/ppermute | solution.py:54
  66.9 9.1 %collective-permute-done.7 = bf16[72,1152]{1,0:T(8,128)(2,1)S(1)} collective-permute-done((bf16[72,1152]{1,0:T(8,128)(2,1)S(1)}, bf16[72,1152]{1,0:T(8,128)(2,1)S(1)}, u32[]{:S(2)}, u32[]{:S(2)}) %collective-permute-start.7) | collective-permute-done | bytes 165920 | tf_op jit(solution)/shard_map/ppermute | solution.py:54
  76.0 7.8 %collective-permute-done.8 = bf16[72,1152]{1,0:T(8,128)(2,1)S(1)} collective-permute-done((bf16[72,1152]{1,0:T(8,128)(2,1)S(1)}, bf16[72,1152]{1,0:T(8,128)(2,1)S(1)}, u32[]{:S(2)}, u32[]{:S(2)}) %collective-permute-start.8) | collective-permute-done | bytes 165920 | tf_op jit(solution)/shard_map/ppermute | solution.py:54
  83.8 7.6 %collective-permute-done.9 = bf16[72,1152]{1,0:T(8,128)(2,1)S(1)} collective-permute-done((bf16[72,1152]{1,0:T(8,128)(2,1)S(1)}, bf16[72,1152]{1,0:T(8,128)(2,1)S(1)}, u32[]{:S(2)}, u32[]{:S(2)}) %collective-permute-start.9) | collective-permute-done | bytes 165920 | tf_op jit(solution)/shard_map/ppermute | solution.py:54
  91.4 8.7 %collective-permute-done.10 = bf16[72,1152]{1,0:T(8,128)(2,1)S(1)} collective-permute-done((bf16[72,1152]{1,0:T(8,128)(2,1)S(1)}, bf16[72,1152]{1,0:T(8,128)(2,1)S(1)}, u32[]{:S(2)}, u32[]{:S(2)}) %collective-permute-start.10) | collective-permute-done | bytes 165920 | tf_op jit(solution)/shard_map/ppermute | solution.py:54
  100.1 7.7 %collective-permute-done.11 = bf16[72,1152]{1,0:T(8,128)(2,1)S(1)} collective-permute-done((bf16[72,1152]{1,0:T(8,128)(2,1)S(1)}, bf16[72,1152]{1,0:T(8,128)(2,1)S(1)}, u32[]{:S(2)}, u32[]{:S(2)}) %collective-permute-start.11) | collective-permute-done | bytes 165920 | tf_op jit(solution)/shard_map/ppermute | solution.py:54
  107.9 7.5 %collective-permute-done.12 = bf16[72,1152]{1,0:T(8,128)(2,1)S(1)} collective-permute-done((bf16[72,1152]{1,0:T(8,128)(2,1)S(1)}, bf16[72,1152]{1,0:T(8,128)(2,1)S(1)}, u32[]{:S(2)}, u32[]{:S(2)}) %collective-permute-start.12) | collective-permute-done | bytes 165920 | tf_op jit(solution)/shard_map/ppermute | solution.py:54
  115.3 7.5 %collective-permute-done.13 = bf16[72,1152]{1,0:T(8,128)(2,1)S(1)} collective-permute-done((bf16[72,1152]{1,0:T(8,128)(2,1)S(1)}, bf16[72,1152]{1,0:T(8,128)(2,1)S(1)}, u32[]{:S(2)}, u32[]{:S(2)}) %collective-permute-start.13) | collective-permute-done | bytes 165920 | tf_op jit(solution)/shard_map/ppermute | solution.py:54
  122.9 7.3 %collective-permute-done.14 = bf16[72,1152]{1,0:T(8,128)(2,1)S(1)} collective-permute-done((bf16[72,1152]{1,0:T(8,128)(2,1)S(1)}, bf16[72,1152]{1,0:T(8,128)(2,1)S(1)}, u32[]{:S(2)}, u32[]{:S(2)}) %collective-permute-start.14) | collective-permute-done | bytes 165920 | tf_op jit(solution)/shard_map/ppermute | solution.py:54
  131.1 0.9 fusion.11
  132.2 0.9 reshape.43
  133.2 2.3 convolution_convert_fusion.4
  135.6 0.9 reshape.44
  136.5 2.4 convolution_convert_fusion.6
  138.9 0.9 reshape.40
  139.9 27.5 %all-gather.6.cloned.1.call-done = bf16[1152,1152]{1,0:T(8,128)(2,1)} async-done(((bf16[72,1152]{1,0:T(8,128)(2,1)}), bf16[1152,1152]{1,0:T(8,128)(2,1)}) %all-gather.6.cloned.1.call-update) | async-done | bytes 2654224 | tf_op jit(solution)/shard_map/all_gather | solution.py:30
  167.3 2.3 convolution_convert_fusion.5
  169.7 1.8 reshape.41
  171.8 2.7 fusion.57
  174.6 3.0 fusion.20
  177.6 3.1 fusion.21
  180.7 2.4 fusion.22
  183.0 1.6 fusion.23
  185.3 1.2 copy.44
  187.0 1.2 copy.46
  188.8 0.5 convert_element_type.89
  189.3 0.9 convolution_convert_fusion
  190.2 1.1 fusion.4
  191.4 0.9 fusion.3
  192.3 0.9 fusion.2
  193.1 28.0 %pad_maximum_fusion = bf16[1152,4608]{0,1:T(8,128)(2,1)} fusion(bf16[1152,1152]{0,1:T(8,128)(2,1)S(1)} %convolution_convert_fusion, bf16[1152,1152]{0,1:T(8,128)(2,1)S(1)} %fusion.4, bf16[1152,1152]{0,1:T(8,128)(2,1)S(1)} %fusion.3, bf16[1152,1152]{0,1:T(8,128)(2,1)S(1)} %fusion.2), kind=kLoop, calls=%fused_computation.2 | loop fusion | flops 42467328 | bytes 21233664 | tf_op jit(solution)/shard_map/concatenate | solution.py:80
  221.1 15.3 %copy.53 = bf16[1152,4608]{1,0:T(8,128)(2,1)} copy(bf16[1152,4608]{0,1:T(8,128)(2,1)} %pad_maximum_fusion) | data formatting | bytes 21233664
  236.5 2.8 fusion.62
  239.3 0.9 convolution_add_fusion.1
  240.3 1.6 fusion.7
  241.9 114.3 %reduce-scatter.4.cloned.1.call-done = bf16[72,4608]{1,0:T(8,128)(2,1)} async-done(((bf16[1152,4608]{1,0:T(8,128)(2,1)}), bf16[72,4608]{1,0:T(8,128)(2,1)}) %reduce-scatter.4.cloned.1.call-update) | async-done | bytes 663568
  356.2 2.3 copy.54
  358.5 57.9 %all-reduce.1 = f32[72,4608]{0,1:T(8,128)S(1)} all-reduce(bf16[72,4608]{0,1:T(8,128)(2,1)} %copy.54), channel_id=1, replica_groups=mesh['pix'=16,'rep'=2] {'rep'}, use_global_device_ids=true, to_apply=%region_4.5 | all-reduce | flops 331776 | bytes 1990656 | tf_op jit(solution)/shard_map/psum | solution.py:106
  416.4 1.7 copy.50
  (77 shorter events, 3.4 us)
Async XLA Ops:
  7.2 126.1 %copy-start = (bf16[8,16,1152]{2,1,0:T(8,128)(2,1)S(1)}, bf16[8,16,1152]{2,1,0:T(8,128)(2,1)}, u32[]{:S(2)}) copy-start(bf16[8,16,1152]{2,1,0:T(8,128)(2,1)} %param.6) | copy-start | bytes 884740
  7.2 123.5 %copy-start.6 = (bf16[72,1152]{1,0:T(8,128)(2,1)S(1)}, bf16[72,1152]{1,0:T(8,128)(2,1)}, u32[]{:S(2)}) copy-start(bf16[72,1152]{1,0:T(8,128)(2,1)} %param.11) | copy-start | bytes 497668
  7.2 126.0 %all-gather.8.cloned.1.call-start = ((), (), s32[]{:S(2)}) async-start(), calls=%async_computation.3 | async-start | bytes 2820096 | tf_op jit(solution)/shard_map/all_gather | solution.py:32
  7.9 128.6 %all-gather.4.cloned.1.call-start = ((), (), s32[]{:S(2)}) async-start(), calls=%async_computation.1 | async-start | bytes 2820096 | tf_op jit(solution)/shard_map/all_gather | solution.py:31
  8.7 158.6 %all-gather.6.cloned.1.call-start = ((), (), s32[]{:S(2)}) async-start(), calls=%async_computation.2 | async-start | bytes 2820096 | tf_op jit(solution)/shard_map/all_gather | solution.py:30
  8.7 8.7 %collective-permute-start = (bf16[72,1152]{1,0:T(8,128)(2,1)}, bf16[72,1152]{1,0:T(8,128)(2,1)S(1)}, u32[]{:S(2)}, u32[]{:S(2)}) collective-permute-start(bf16[72,1152]{1,0:T(8,128)(2,1)} %param.11), channel_id=1, source_target_pairs={{0,2},{2,4},{4,6},{6,8},{8,10},{10,12},{12,14},{14,16},{16,18},{18... | collective-permute-start | bytes 497672 | tf_op jit(solution)/shard_map/ppermute | solution.py:54
  17.5 7.6 %collective-permute-start.1 = (bf16[72,1152]{1,0:T(8,128)(2,1)S(1)}, bf16[72,1152]{1,0:T(8,128)(2,1)S(1)}, u32[]{:S(2)}, u32[]{:S(2)}) collective-permute-start(bf16[72,1152]{1,0:T(8,128)(2,1)S(1)} %collective-permute-done), channel_id=1, source_target_pairs={{0,2},{2,4},{4,6},{6,8},{8,10},{10,12},{12,14},{14,16},{16,18},{18... | collective-permute-start | bytes 497672 | tf_op jit(solution)/shard_map/ppermute | solution.py:54
  25.0 8.8 %collective-permute-start.2 = (bf16[72,1152]{1,0:T(8,128)(2,1)S(1)}, bf16[72,1152]{1,0:T(8,128)(2,1)S(1)}, u32[]{:S(2)}, u32[]{:S(2)}) collective-permute-start(bf16[72,1152]{1,0:T(8,128)(2,1)S(1)} %collective-permute-done.1), channel_id=1, source_target_pairs={{0,2},{2,4},{4,6},{6,8},{8,10},{10,12},{12,14},{14,16},{16,18},{18... | collective-permute-start | bytes 497672 | tf_op jit(solution)/shard_map/ppermute | solution.py:54
  33.8 7.5 %collective-permute-start.3 = (bf16[72,1152]{1,0:T(8,128)(2,1)S(1)}, bf16[72,1152]{1,0:T(8,128)(2,1)S(1)}, u32[]{:S(2)}, u32[]{:S(2)}) collective-permute-start(bf16[72,1152]{1,0:T(8,128)(2,1)S(1)} %collective-permute-done.2), channel_id=1, source_target_pairs={{0,2},{2,4},{4,6},{6,8},{8,10},{10,12},{12,14},{14,16},{16,18},{18... | collective-permute-start | bytes 497672 | tf_op jit(solution)/shard_map/ppermute | solution.py:54
  41.3 10.0 %collective-permute-start.4 = (bf16[72,1152]{1,0:T(8,128)(2,1)S(1)}, bf16[72,1152]{1,0:T(8,128)(2,1)S(1)}, u32[]{:S(2)}, u32[]{:S(2)}) collective-permute-start(bf16[72,1152]{1,0:T(8,128)(2,1)S(1)} %collective-permute-done.3), channel_id=1, source_target_pairs={{0,2},{2,4},{4,6},{6,8},{8,10},{10,12},{12,14},{14,16},{16,18},{18... | collective-permute-start | bytes 497672 | tf_op jit(solution)/shard_map/ppermute | solution.py:54
  51.3 8.2 %collective-permute-start.5 = (bf16[72,1152]{1,0:T(8,128)(2,1)S(1)}, bf16[72,1152]{1,0:T(8,128)(2,1)S(1)}, u32[]{:S(2)}, u32[]{:S(2)}) collective-permute-start(bf16[72,1152]{1,0:T(8,128)(2,1)S(1)} %collective-permute-done.4), channel_id=1, source_target_pairs={{0,2},{2,4},{4,6},{6,8},{8,10},{10,12},{12,14},{14,16},{16,18},{18... | collective-permute-start | bytes 497672 | tf_op jit(solution)/shard_map/ppermute | solution.py:54
  59.5 7.5 %collective-permute-start.6 = (bf16[72,1152]{1,0:T(8,128)(2,1)S(1)}, bf16[72,1152]{1,0:T(8,128)(2,1)S(1)}, u32[]{:S(2)}, u32[]{:S(2)}) collective-permute-start(bf16[72,1152]{1,0:T(8,128)(2,1)S(1)} %collective-permute-done.5), channel_id=1, source_target_pairs={{0,2},{2,4},{4,6},{6,8},{8,10},{10,12},{12,14},{14,16},{16,18},{18... | collective-permute-start | bytes 497672 | tf_op jit(solution)/shard_map/ppermute | solution.py:54
  66.9 9.1 %collective-permute-start.7 = (bf16[72,1152]{1,0:T(8,128)(2,1)S(1)}, bf16[72,1152]{1,0:T(8,128)(2,1)S(1)}, u32[]{:S(2)}, u32[]{:S(2)}) collective-permute-start(bf16[72,1152]{1,0:T(8,128)(2,1)S(1)} %collective-permute-done.6), channel_id=1, source_target_pairs={{0,2},{2,4},{4,6},{6,8},{8,10},{10,12},{12,14},{14,16},{16,18},{18... | collective-permute-start | bytes 497672 | tf_op jit(solution)/shard_map/ppermute | solution.py:54
  76.0 7.8 %collective-permute-start.8 = (bf16[72,1152]{1,0:T(8,128)(2,1)S(1)}, bf16[72,1152]{1,0:T(8,128)(2,1)S(1)}, u32[]{:S(2)}, u32[]{:S(2)}) collective-permute-start(bf16[72,1152]{1,0:T(8,128)(2,1)S(1)} %collective-permute-done.7), channel_id=1, source_target_pairs={{0,2},{2,4},{4,6},{6,8},{8,10},{10,12},{12,14},{14,16},{16,18},{18... | collective-permute-start | bytes 497672 | tf_op jit(solution)/shard_map/ppermute | solution.py:54
  83.8 7.6 %collective-permute-start.9 = (bf16[72,1152]{1,0:T(8,128)(2,1)S(1)}, bf16[72,1152]{1,0:T(8,128)(2,1)S(1)}, u32[]{:S(2)}, u32[]{:S(2)}) collective-permute-start(bf16[72,1152]{1,0:T(8,128)(2,1)S(1)} %collective-permute-done.8), channel_id=1, source_target_pairs={{0,2},{2,4},{4,6},{6,8},{8,10},{10,12},{12,14},{14,16},{16,18},{18... | collective-permute-start | bytes 497672 | tf_op jit(solution)/shard_map/ppermute | solution.py:54
  91.4 8.7 %collective-permute-start.10 = (bf16[72,1152]{1,0:T(8,128)(2,1)S(1)}, bf16[72,1152]{1,0:T(8,128)(2,1)S(1)}, u32[]{:S(2)}, u32[]{:S(2)}) collective-permute-start(bf16[72,1152]{1,0:T(8,128)(2,1)S(1)} %collective-permute-done.9), channel_id=1, source_target_pairs={{0,2},{2,4},{4,6},{6,8},{8,10},{10,12},{12,14},{14,16},{16,18},{18... | collective-permute-start | bytes 497672 | tf_op jit(solution)/shard_map/ppermute | solution.py:54
  100.1 7.7 %collective-permute-start.11 = (bf16[72,1152]{1,0:T(8,128)(2,1)S(1)}, bf16[72,1152]{1,0:T(8,128)(2,1)S(1)}, u32[]{:S(2)}, u32[]{:S(2)}) collective-permute-start(bf16[72,1152]{1,0:T(8,128)(2,1)S(1)} %collective-permute-done.10), channel_id=1, source_target_pairs={{0,2},{2,4},{4,6},{6,8},{8,10},{10,12},{12,14},{14,16},{16,18},{18... | collective-permute-start | bytes 497672 | tf_op jit(solution)/shard_map/ppermute | solution.py:54
  107.9 7.5 %collective-permute-start.12 = (bf16[72,1152]{1,0:T(8,128)(2,1)S(1)}, bf16[72,1152]{1,0:T(8,128)(2,1)S(1)}, u32[]{:S(2)}, u32[]{:S(2)}) collective-permute-start(bf16[72,1152]{1,0:T(8,128)(2,1)S(1)} %collective-permute-done.11), channel_id=1, source_target_pairs={{0,2},{2,4},{4,6},{6,8},{8,10},{10,12},{12,14},{14,16},{16,18},{18... | collective-permute-start | bytes 497672 | tf_op jit(solution)/shard_map/ppermute | solution.py:54
  115.3 7.5 %collective-permute-start.13 = (bf16[72,1152]{1,0:T(8,128)(2,1)S(1)}, bf16[72,1152]{1,0:T(8,128)(2,1)S(1)}, u32[]{:S(2)}, u32[]{:S(2)}) collective-permute-start(bf16[72,1152]{1,0:T(8,128)(2,1)S(1)} %collective-permute-done.12), channel_id=1, source_target_pairs={{0,2},{2,4},{4,6},{6,8},{8,10},{10,12},{12,14},{14,16},{16,18},{18... | collective-permute-start | bytes 497672 | tf_op jit(solution)/shard_map/ppermute | solution.py:54
  122.8 7.5 %collective-permute-start.14 = (bf16[72,1152]{1,0:T(8,128)(2,1)S(1)}, bf16[72,1152]{1,0:T(8,128)(2,1)S(1)}, u32[]{:S(2)}, u32[]{:S(2)}) collective-permute-start(bf16[72,1152]{1,0:T(8,128)(2,1)S(1)} %collective-permute-done.13), channel_id=1, source_target_pairs={{0,2},{2,4},{4,6},{6,8},{8,10},{10,12},{12,14},{14,16},{16,18},{18... | collective-permute-start | bytes 497672 | tf_op jit(solution)/shard_map/ppermute | solution.py:54
  122.8 233.4 %reduce-scatter.4.cloned.1.call-start = ((), (), s32[]{:S(2)}) async-start(), calls=%async_computation.4 | async-start | bytes 11280384
  122.9 8.2 %copy-start.5 = (bf16[8,16,1152]{2,1,0:T(8,128)(2,1)S(1)}, bf16[8,16,1152]{2,1,0:T(8,128)(2,1)}, u32[]{:S(2)}) copy-start(bf16[8,16,1152]{2,1,0:T(8,128)(2,1)} %param.7) | copy-start | bytes 884740
  180.6 4.0 copy-start.7
  188.7 3.6 copy-start.3
  236.5 2.9 copy-start.1
  236.5 3.8 copy-start.2
  236.5 3.8 copy-start.4
Sparse Core Ops, SparseCore 0:
  10.1 47.4 all-gather.7
  59.8 46.3 all-gather.3
  122.9 44.3 all-gather.5
  236.6 119.5 reduce-scatter.3
